TPU v7x, 32 devices: a whole 2x2x4 slice. The times are simulated.
32 devices in a mesh: dp: 8 (over y, x, core), tensor: 4 (over z).
Axes of the slice: x: 2, y: 2, z: 4, core: 2. Of those that a mesh axis runs over, the one named last changes fastest.
Arguments:
- inputs: bfloat16 [8, 1024, 2048], P('dp', 'tensor'), may hold values from -6 to 6
- teacher: bfloat16 [8, 1024, 2048], P('dp', 'tensor'), may hold values from -6 to 6
- lengths: int32 [8], P('dp'), may hold values from 1 to 1024, 5120 in all
- w_query: bfloat16 [2048, 2048], P('dp', 'tensor'), may hold values from -0.1875 to 0.1875
- w_key: bfloat16 [2048, 2048], P('dp', 'tensor'), may hold values from -0.1875 to 0.1875
- w_value: bfloat16 [2048, 2048], P('dp', 'tensor'), may hold values from -0.125 to 0.125
- w_out: bfloat16 [2048, 2048], P('tensor', 'dp'), may hold values from -2 to 2
- w_gate: bfloat16 [2048, 8192], P('dp', 'tensor'), may hold values from -0.125 to 0.125
- w_up: bfloat16 [2048, 8192], P('dp', 'tensor'), may hold values from -0.125 to 0.125
- w_down: bfloat16 [8192, 2048], P('tensor', 'dp'), may hold values from -0.0625 to 0.0625
Outputs:
- output: bfloat16 [8, 1024, 2048], P('dp', 'tensor')
- loss: float32 [], replicated
- grad_input: float32 [8, 1024, 2048], P('dp', 'tensor')
- grad_query: float32 [2048, 2048], P('dp', 'tensor')
- grad_key: float32 [2048, 2048], P('dp', 'tensor')
- grad_value: float32 [2048, 2048], P('dp', 'tensor')
- grad_out: float32 [2048, 2048], P('tensor', 'dp')
- grad_gate: float32 [2048, 8192], P('dp', 'tensor')
- grad_up: float32 [2048, 8192], P('dp', 'tensor')
- grad_down: float32 [8192, 2048], P('tensor', 'dp')
Inputs may be any that keep to these rules, and one draw needn't show every extreme that they name: Sequence s holds lengths[s] valid tokens at its start; its other slots of 1024 are padding; some sequence fills all 1024 slots and the lengths add up to 5120.
All inputs are finite; a program needn't handle non-finite values. No bound on the sum of `lengths` on one device may be relied on, other than what follows from the above.
Results may differ from a plain program's by a relative error of at most 0.015.
The roundings to bfloat16 on the way count: a program that leaves them out, or rounds other values in their place, can miss the bound.
Values may be sent and summed in bfloat16 or wider, within the bound.
No kernel may reach another device: no remote copies, remote signals or barrier semaphores. Data moves between devices by JAX's collectives and lax.ppermute only.
A program may use at most 192 MiB of HBM per device.

v0:
```python
import math
import jax
import jax.numpy as jnp
from jax import lax
from jax.sharding import PartitionSpec as P

HS = 128
EPSILON = 1e-05


def layer_norm(values):
    centre = values - jnp.mean(values, axis=-1, keepdims=True)
    spread = jnp.mean(centre * centre, axis=-1, keepdims=True)
    return centre * lax.rsqrt(spread + EPSILON)


def norm_back(values, grad_in):
    centre = values - jnp.mean(values, axis=-1, keepdims=True)
    spread = jnp.mean(centre * centre, axis=-1, keepdims=True)
    inverse = lax.rsqrt(spread + EPSILON)
    normed = centre * inverse
    return inverse * (
        grad_in
        - jnp.mean(grad_in, axis=-1, keepdims=True)
        - normed * jnp.mean(grad_in * normed, axis=-1, keepdims=True)
    )


def rotary_tables(length, size):
    half_size = size // 2
    inverse = jnp.exp(jnp.arange(half_size, dtype=jnp.float32) * (-2.0 * math.log(10000.0) / size))
    angles = jnp.arange(length, dtype=jnp.float32)[:, None] * inverse[None, :]
    return (jnp.cos(angles), jnp.sin(angles))


def rotate(values, cosine_table, sine_table):
    half_size = values.shape[-1] // 2
    first_half = values[..., :half_size]
    second_half = values[..., half_size:]
    cosine_rows = cosine_table[:, None, :]
    sine_rows = sine_table[:, None, :]
    return jnp.concatenate(
        [
            first_half * cosine_rows - second_half * sine_rows,
            second_half * cosine_rows + first_half * sine_rows,
        ],
        axis=-1,
    )


def rotate_back(grads, cosine_table, sine_table):
    half_size = grads.shape[-1] // 2
    first_half = grads[..., :half_size]
    second_half = grads[..., half_size:]
    cosine_rows = cosine_table[:, None, :]
    sine_rows = sine_table[:, None, :]
    return jnp.concatenate(
        [
            first_half * cosine_rows + second_half * sine_rows,
            second_half * cosine_rows - first_half * sine_rows,
        ],
        axis=-1,
    )


def local(inputs, teacher, lengths, w_query, w_key, w_value, w_out, w_gate, w_up, w_down):
    tensor_count = lax.axis_size("tensor")
    local_rows = inputs.shape[1]
    slot_count = local_rows * tensor_count
    token_total = slot_count * lax.axis_size("dp")
    width_all = inputs.shape[2]
    rows_in = inputs[0].astype(jnp.float32)
    target = teacher[0].astype(jnp.float32)
    own_length = lengths[0]
    positions = lax.axis_index("tensor") * local_rows + jnp.arange(local_rows, dtype=jnp.int32)
    valid_rows = (positions < own_length)[:, None]
    valid_total = lax.psum(own_length.astype(jnp.float32), "dp")
    gathered = (
        lax.all_gather(w_query, "dp", axis=0, tiled=True),
        lax.all_gather(w_key, "dp", axis=0, tiled=True),
        lax.all_gather(w_value, "dp", axis=0, tiled=True),
        lax.all_gather(w_gate, "dp", axis=0, tiled=True),
        lax.all_gather(w_up, "dp", axis=0, tiled=True),
        lax.all_gather(w_out, "dp", axis=1, tiled=True),
        lax.all_gather(w_down, "dp", axis=1, tiled=True),
    )
    query_full, key_full, value_full, gate_full, up_full, out_full, down_full = gathered
    head_cols = query_full.shape[1]
    head_count = head_cols // HS
    cosine_table, sine_table = rotary_tables(slot_count, HS)
    query_scale = HS ** (-0.5)
    block_rows = min(slot_count, 512)
    block_count = slot_count // block_rows
    key_index = jnp.arange(slot_count, dtype=jnp.int32)
    normed = layer_norm(rows_in).astype(jnp.bfloat16)
    features = lax.all_gather(normed, "tensor", axis=0, tiled=True)
    queries = jnp.dot(features, query_full, preferred_element_type=jnp.float32)
    key_raw = jnp.dot(features, key_full, preferred_element_type=jnp.float32)
    value_raw = jnp.dot(features, value_full, preferred_element_type=jnp.float32)
    query_rot = (
        rotate(queries.reshape(slot_count, head_count, HS), cosine_table, sine_table) * query_scale
    ).astype(jnp.bfloat16)
    key_rot = rotate(key_raw.reshape(slot_count, head_count, HS), cosine_table, sine_table).astype(
        jnp.bfloat16
    )
    value_heads = value_raw.reshape(slot_count, head_count, HS).astype(jnp.bfloat16)

    def block_scores(block):
        start = block * block_rows
        query_rows = query_rot[start : start + block_rows]
        scores = jnp.einsum("qhd,khd->hqk", query_rows, key_rot, preferred_element_type=jnp.float32)
        causal = (start + jnp.arange(block_rows, dtype=jnp.int32))[:, None] >= key_index[None, :]
        return (jnp.where(causal[None], scores, -1e30), query_rows)

    mixed_blocks = []
    lse_blocks = []
    for block in range(block_count):
        scores, query_rows = block_scores(block)
        largest = jnp.max(scores, axis=-1, keepdims=True)
        shifted = jnp.exp(scores - largest)
        totals = jnp.sum(shifted, axis=-1, keepdims=True)
        attention = shifted / totals
        lse_blocks.append(largest + jnp.log(totals))
        mixed_blocks.append(
            jnp.einsum(
                "hqk,khd->qhd",
                attention.astype(jnp.bfloat16),
                value_heads,
                preferred_element_type=jnp.float32,
            )
        )
    attended = (
        jnp.concatenate(mixed_blocks, axis=0).reshape(slot_count, head_cols).astype(jnp.bfloat16)
    )
    attn_out = lax.psum_scatter(
        jnp.dot(attended, out_full, preferred_element_type=jnp.float32),
        "tensor",
        scatter_dimension=0,
        tiled=True,
    )
    residual = rows_in + attn_out
    normed_two = layer_norm(residual).astype(jnp.bfloat16)
    features_two = lax.all_gather(normed_two, "tensor", axis=0, tiled=True)
    gate_pre = jnp.dot(features_two, gate_full, preferred_element_type=jnp.float32)
    up_pre = jnp.dot(features_two, up_full, preferred_element_type=jnp.float32)
    gate_sigmoid = jax.nn.sigmoid(gate_pre)
    activated = gate_pre * gate_sigmoid
    hidden = (activated * up_pre).astype(jnp.bfloat16)
    mlp_out = lax.psum_scatter(
        jnp.dot(hidden, down_full, preferred_element_type=jnp.float32).astype(jnp.bfloat16),
        "tensor",
        scatter_dimension=0,
        tiled=True,
    ).astype(jnp.float32)
    result = residual + mlp_out
    errors = jnp.where(valid_rows, result - target, 0.0)
    squares = jnp.sum(errors * errors)
    total_squares = lax.psum(squares, ("dp", "tensor"))
    loss_value = total_squares / (valid_total * width_all)
    grad_result = errors * (token_total / valid_total)
    regathered = (
        lax.all_gather(w_query, "dp", axis=0, tiled=True),
        lax.all_gather(w_key, "dp", axis=0, tiled=True),
        lax.all_gather(w_value, "dp", axis=0, tiled=True),
        lax.all_gather(w_gate, "dp", axis=0, tiled=True),
        lax.all_gather(w_up, "dp", axis=0, tiled=True),
        lax.all_gather(w_out, "dp", axis=1, tiled=True),
        lax.all_gather(w_down, "dp", axis=1, tiled=True),
    )
    query_full, key_full, value_full, gate_full, up_full, out_full, down_full = regathered
    down_grad_in = lax.all_gather(grad_result.astype(jnp.bfloat16), "tensor", axis=0, tiled=True)
    grad_down = jnp.einsum("tf,td->fd", hidden, down_grad_in, preferred_element_type=jnp.float32)
    hidden_grad = jnp.einsum(
        "td,fd->tf", down_grad_in, down_full, preferred_element_type=jnp.float32
    )
    gate_grad = (
        hidden_grad * up_pre * gate_sigmoid * (1.0 + gate_pre * (1.0 - gate_sigmoid))
    ).astype(jnp.bfloat16)
    up_grad = (hidden_grad * activated).astype(jnp.bfloat16)
    grad_gate = jnp.einsum("td,tf->df", features_two, gate_grad, preferred_element_type=jnp.float32)
    grad_up = jnp.einsum("td,tf->df", features_two, up_grad, preferred_element_type=jnp.float32)
    feature_grad = jnp.einsum(
        "tf,df->td", gate_grad, gate_full, preferred_element_type=jnp.float32
    ) + jnp.einsum("tf,df->td", up_grad, up_full, preferred_element_type=jnp.float32)
    normed_two_grad = lax.psum_scatter(
        feature_grad.astype(jnp.bfloat16), "tensor", scatter_dimension=0, tiled=True
    ).astype(jnp.float32)
    residual_grad = grad_result + norm_back(residual, normed_two_grad)
    attn_grad_in = lax.all_gather(residual_grad.astype(jnp.bfloat16), "tensor", axis=0, tiled=True)
    grad_out = jnp.einsum("tc,td->cd", attended, attn_grad_in, preferred_element_type=jnp.float32)
    mixed_grad = (
        jnp.einsum("td,cd->tc", attn_grad_in, out_full, preferred_element_type=jnp.float32)
        .astype(jnp.bfloat16)
        .reshape(slot_count, head_count, HS)
    )
    value_grad = jnp.zeros((slot_count, head_count, HS), jnp.float32)
    key_grad = jnp.zeros((slot_count, head_count, HS), jnp.float32)
    query_parts = []
    for block in range(block_count):
        scores, query_rows = block_scores(block)
        attention = jnp.exp(scores - lse_blocks[block])
        start = block * block_rows
        mixed_rows = mixed_grad[start : start + block_rows]
        value_grad = value_grad + jnp.einsum(
            "hqk,qhd->khd",
            attention.astype(jnp.bfloat16),
            mixed_rows,
            preferred_element_type=jnp.float32,
        )
        prob_grad = jnp.einsum(
            "qhd,khd->hqk", mixed_rows, value_heads, preferred_element_type=jnp.float32
        )
        score_grad = (
            attention * (prob_grad - jnp.sum(prob_grad * attention, axis=-1, keepdims=True))
        ).astype(jnp.bfloat16)
        query_parts.append(
            jnp.einsum("hqk,khd->qhd", score_grad, key_rot, preferred_element_type=jnp.float32)
        )
        key_grad = key_grad + jnp.einsum(
            "hqk,qhd->khd", score_grad, query_rows, preferred_element_type=jnp.float32
        )
    query_grad = (
        (rotate_back(jnp.concatenate(query_parts, axis=0), cosine_table, sine_table) * query_scale)
        .astype(jnp.bfloat16)
        .reshape(slot_count, head_cols)
    )
    key_grad_low = (
        rotate_back(key_grad, cosine_table, sine_table)
        .astype(jnp.bfloat16)
        .reshape(slot_count, head_cols)
    )
    value_grad_low = value_grad.astype(jnp.bfloat16).reshape(slot_count, head_cols)
    grad_query = jnp.einsum("td,tc->dc", features, query_grad, preferred_element_type=jnp.float32)
    grad_key = jnp.einsum("td,tc->dc", features, key_grad_low, preferred_element_type=jnp.float32)
    grad_value = jnp.einsum(
        "td,tc->dc", features, value_grad_low, preferred_element_type=jnp.float32
    )
    features_grad = (
        jnp.einsum("tc,dc->td", query_grad, query_full, preferred_element_type=jnp.float32)
        + jnp.einsum("tc,dc->td", key_grad_low, key_full, preferred_element_type=jnp.float32)
        + jnp.einsum("tc,dc->td", value_grad_low, value_full, preferred_element_type=jnp.float32)
    )
    normed_grad = lax.psum_scatter(
        features_grad.astype(jnp.bfloat16), "tensor", scatter_dimension=0, tiled=True
    ).astype(jnp.float32)
    input_grad = residual_grad + norm_back(rows_in, normed_grad)
    summed = (
        lax.psum_scatter(
            grad_query.astype(jnp.bfloat16), "dp", scatter_dimension=0, tiled=True
        ).astype(jnp.float32),
        lax.psum_scatter(
            grad_key.astype(jnp.bfloat16), "dp", scatter_dimension=0, tiled=True
        ).astype(jnp.float32),
        lax.psum_scatter(
            grad_value.astype(jnp.bfloat16), "dp", scatter_dimension=0, tiled=True
        ).astype(jnp.float32),
        lax.psum_scatter(
            grad_gate.astype(jnp.bfloat16), "dp", scatter_dimension=0, tiled=True
        ).astype(jnp.float32),
        lax.psum_scatter(
            grad_up.astype(jnp.bfloat16), "dp", scatter_dimension=0, tiled=True
        ).astype(jnp.float32),
        lax.psum_scatter(
            grad_out.astype(jnp.bfloat16), "dp", scatter_dimension=1, tiled=True
        ).astype(jnp.float32),
        lax.psum_scatter(
            grad_down.astype(jnp.bfloat16), "dp", scatter_dimension=1, tiled=True
        ).astype(jnp.float32),
    )
    return (
        result.astype(jnp.bfloat16)[None],
        loss_value,
        input_grad[None],
        summed[0],
        summed[1],
        summed[2],
        summed[5],
        summed[3],
        summed[4],
        summed[6],
    )


def solution(mesh):
    in_specs = (
        P("dp", "tensor", None),
        P("dp", "tensor", None),
        P("dp"),
        P("dp", "tensor"),
        P("dp", "tensor"),
        P("dp", "tensor"),
        P("tensor", "dp"),
        P("dp", "tensor"),
        P("dp", "tensor"),
        P("tensor", "dp"),
    )
    out_specs = (
        P("dp", "tensor", None),
        P(),
        P("dp", "tensor", None),
        P("dp", "tensor"),
        P("dp", "tensor"),
        P("dp", "tensor"),
        P("tensor", "dp"),
        P("dp", "tensor"),
        P("dp", "tensor"),
        P("tensor", "dp"),
    )
    return jax.shard_map(local, mesh=mesh, in_specs=in_specs, out_specs=out_specs, check_vma=False)
```

profile of v0, /device:TPU:0, one launch (start us, length us, event | category | flops | bytes accessed | tf_op | source)
XLA Modules:
  0.0 1495.9 jit_solution(12879193869445910565)
XLA Ops:
  19.6 21.0 %all-gather.18.cloned.1.call-done = bf16[2048,512]{1,0:T(8,128)(2,1)} async-done(((bf16[256,512]{1,0:T(8,128)(2,1)}), bf16[2048,512]{1,0:T(8,128)(2,1)}) %all-gather.18.cloned.1.call-update) | async-done | bytes 2097168 | tf_op jit(solution)/shard_map/all_gather | solution.py:80
  40.5 82.9 %all-gather.12.cloned.1.call-done = bf16[1024,2048]{1,0:T(8,128)(2,1)} async-done(((bf16[256,2048]{1,0:T(8,128)(2,1)}), bf16[1024,2048]{1,0:T(8,128)(2,1)}) %all-gather.12.cloned.1.call-update) | async-done | bytes 4194320 | tf_op jit(solution)/shard_map/all_gather | solution.py:96
  135.3 16.5 %all-gather.16.cloned.1.call-done = bf16[2048,512]{1,0:T(8,128)(2,1)} async-done(((bf16[256,512]{1,0:T(8,128)(2,1)}), bf16[2048,512]{1,0:T(8,128)(2,1)}) %all-gather.16.cloned.1.call-update) | async-done | bytes 2097168 | tf_op jit(solution)/shard_map/all_gather | solution.py:79
  192.4 19.1 %all-gather.20.cloned.1.call-done = bf16[512,2048]{1,0:T(8,128)(2,1)} async-done(((bf16[512,256]{1,0:T(8,128)(2,1)}), bf16[512,2048]{1,0:T(8,128)(2,1)}) %all-gather.20.cloned.1.call-update) | async-done | bytes 2097168 | tf_op jit(solution)/shard_map/all_gather | solution.py:84
  219.6 143.8 %reduce-scatter.12.cloned.1.call-done = f32[256,2048]{1,0:T(8,128)} async-done(((f32[1024,2048]{1,0:T(8,128)}), f32[256,2048]{1,0:T(8,128)}) %reduce-scatter.12.cloned.1.call-update) | async-done | bytes 2097168 | tf_op jit(solution)/shard_map/reduce_scatter | solution.py:135
  368.3 52.1 %all-gather.24.cloned.1.call-done = bf16[2048,2048]{1,0:T(8,128)(2,1)} async-done(((bf16[256,2048]{1,0:T(8,128)(2,1)}), bf16[2048,2048]{1,0:T(8,128)(2,1)}) %all-gather.24.cloned.1.call-update) | async-done | bytes 8388624 | tf_op jit(solution)/shard_map/all_gather | solution.py:82
  420.4 82.9 %all-gather.22.cloned.1.call-done = bf16[1024,2048]{1,0:T(8,128)(2,1)} async-done(((bf16[256,2048]{1,0:T(8,128)(2,1)}), bf16[1024,2048]{1,0:T(8,128)(2,1)}) %all-gather.22.cloned.1.call-update) | async-done | bytes 4194320 | tf_op jit(solution)/shard_map/all_gather | solution.py:143
  503.3 14.9 fusion.68
  518.2 40.0 %all-gather.26.cloned.1.call-done = bf16[2048,2048]{1,0:T(8,128)(2,1)} async-done(((bf16[256,2048]{1,0:T(8,128)(2,1)}), bf16[2048,2048]{1,0:T(8,128)(2,1)}) %all-gather.26.cloned.1.call-update) | async-done | bytes 8388624 | tf_op jit(solution)/shard_map/all_gather | solution.py:83
  558.2 16.9 %multiply_convert_fusion.4 = (bf16[1024,2048]{1,0:T(8,128)(2,1)}, f32[1024,2048]{1,0:T(8,128)}) fusion(f32[1024,2048]{1,0:T(8,128)} %fusion.68, bf16[1024,2048]{1,0:T(8,128)(2,1)} %all-gather.22.cloned.1.call-done, bf16[2048,2048]{1,0:T(8,128)(2,1)} %all-gather.26.cloned.1.call-done), kind=kOutput, calls=%fused_computation.10 | convolution fusion | flops 8602517504 | bytes 33554432 | tf_op jit(solution)/shard_map/dot_general | solution.py:145
  575.1 40.8 %all-gather.28.cloned.1.call-done = bf16[2048,2048]{1,0:T(8,128)(2,1)} async-done(((bf16[2048,256]{1,0:T(8,128)(2,1)}), bf16[2048,2048]{1,0:T(8,128)(2,1)}) %all-gather.28.cloned.1.call-update) | async-done | bytes 8388624 | tf_op jit(solution)/shard_map/all_gather | solution.py:85
  615.9 13.9 convolution_convert_fusion.3
  630.6 14.0 psum.15
  645.3 61.4 %reduce-scatter.14.cloned.1.call-done = bf16[256,2048]{1,0:T(8,128)(2,1)} async-done(((bf16[1024,2048]{1,0:T(8,128)(2,1)}), bf16[256,2048]{1,0:T(8,128)(2,1)}) %reduce-scatter.14.cloned.1.call-update) | async-done | bytes 1048592 | tf_op jit(solution)/shard_map/reduce_scatter | solution.py:149
  709.5 81.4 %all-gather.30.cloned.1.call-done = bf16[1024,2048]{1,0:T(8,128)(2,1)} async-done(((bf16[256,2048]{1,0:T(8,128)(2,1)}), bf16[1024,2048]{1,0:T(8,128)(2,1)}) %all-gather.30.cloned.1.call-update) | async-done | bytes 4194320 | tf_op jit(solution)/shard_map/all_gather | solution.py:171
  790.9 20.6 %multiply_convert_fusion.2 = (bf16[1024,2048]{1,0:T(8,128)(2,1)}, bf16[1024,2048]{1,0:T(8,128)(2,1)}) fusion(f32[1024,2048]{1,0:T(8,128)} %fusion.68, f32[1024,2048]{1,0:T(8,128)} %get-tuple-element.47, bf16[1024,2048]{1,0:T(8,128)(2,1)} %all-gather.30.cloned.1.call-done, bf16[2048,2048]{1,0:T(8,128)(2,1)} %all-gather.28.cloned.1.call-done), kind=kOutput, calls=%fused_computation.8 | convolution fusion | flops 8617197568 | bytes 37748736 | tf_op jit(solution)/shard_map/td,fd->tf/dot_general | solution.py:173
  811.6 12.7 fusion.69
  824.3 13.1 add_convert_fusion.1
  837.5 75.4 %reduce-scatter.16.cloned.1.call-done = bf16[256,2048]{1,0:T(8,128)(2,1)} async-done(((bf16[1024,2048]{1,0:T(8,128)(2,1)}), bf16[256,2048]{1,0:T(8,128)(2,1)}) %reduce-scatter.16.cloned.1.call-update) | async-done | bytes 1048592 | tf_op jit(solution)/shard_map/reduce_scatter | solution.py:185
  919.7 14.1 convolution_convert_fusion
  933.9 14.5 convolution_convert_fusion.1
  948.5 14.1 convolution_convert_fusion.2
  963.3 37.7 %all-gather.32.cloned.1.call-done = bf16[1024,2048]{1,0:T(8,128)(2,1)} async-done(((bf16[256,2048]{1,0:T(8,128)(2,1)}), bf16[1024,2048]{1,0:T(8,128)(2,1)}) %all-gather.32.cloned.1.call-update) | async-done | bytes 4194320 | tf_op jit(solution)/shard_map/all_gather | solution.py:189
  1035.4 7.9 multiply_reduce_fusion
  1089.3 39.4 %psum.14 = f32[]{:T(128)} all-reduce(f32[]{:T(128)} %get-tuple-element.11), channel_id=1, replica_groups=mesh['dp'=8,'tensor'=4] {'dp','tensor'}, use_global_device_ids=true, to_apply=%region_11.12 | all-reduce | flops 1 | bytes 8 | tf_op jit(solution)/shard_map/psum | solution.py:158
  1132.2 17.7 %reduce-scatter.30.cloned.1.call-done = bf16[256,2048]{1,0:T(8,128)(2,1)} async-done(((bf16[2048,2048]{1,0:T(8,128)(2,1)}), bf16[256,2048]{1,0:T(8,128)(2,1)}) %reduce-scatter.30.cloned.1.call-update) | async-done | bytes 1048592 | tf_op jit(solution)/shard_map/reduce_scatter | solution.py:260
  1152.6 71.8 %reduce-scatter.28.cloned.1.call-done = bf16[256,2048]{1,0:T(8,128)(2,1)} async-done(((bf16[2048,2048]{1,0:T(8,128)(2,1)}), bf16[256,2048]{1,0:T(8,128)(2,1)}) %reduce-scatter.28.cloned.1.call-update) | async-done | bytes 1048592 | tf_op jit(solution)/shard_map/reduce_scatter | solution.py:257
  1227.2 41.9 %reduce-scatter.26.cloned.1.call-done = bf16[512,256]{1,0:T(8,128)(2,1)} async-done(((bf16[512,2048]{1,0:T(8,128)(2,1)}), bf16[512,256]{1,0:T(8,128)(2,1)}) %reduce-scatter.26.cloned.1.call-update) | async-done | bytes 262160 | tf_op jit(solution)/shard_map/reduce_scatter | solution.py:263
  1270.9 42.8 %reduce-scatter.24.cloned.1.call-done = bf16[256,512]{1,0:T(8,128)(2,1)} async-done(((bf16[2048,512]{1,0:T(8,128)(2,1)}), bf16[256,512]{1,0:T(8,128)(2,1)}) %reduce-scatter.24.cloned.1.call-update) | async-done | bytes 262160 | tf_op jit(solution)/shard_map/reduce_scatter | solution.py:254
  1315.5 42.9 %reduce-scatter.20.cloned.1.call-done = bf16[256,512]{1,0:T(8,128)(2,1)} async-done(((bf16[2048,512]{1,0:T(8,128)(2,1)}), bf16[256,512]{1,0:T(8,128)(2,1)}) %reduce-scatter.20.cloned.1.call-update) | async-done | bytes 262160 | tf_op jit(solution)/shard_map/reduce_scatter | solution.py:248
  1360.3 42.8 %reduce-scatter.22.cloned.1.call-done = bf16[256,512]{1,0:T(8,128)(2,1)} async-done(((bf16[2048,512]{1,0:T(8,128)(2,1)}), bf16[256,512]{1,0:T(8,128)(2,1)}) %reduce-scatter.22.cloned.1.call-update) | async-done | bytes 262160 | tf_op jit(solution)/shard_map/reduce_scatter | solution.py:251
  1404.8 77.4 %reduce-scatter.18.cloned.1.call-done = bf16[256,2048]{1,0:T(8,128)(2,1)} async-done(((bf16[1024,2048]{1,0:T(8,128)(2,1)}), bf16[256,2048]{1,0:T(8,128)(2,1)}) %reduce-scatter.18.cloned.1.call-update) | async-done | bytes 1048592 | tf_op jit(solution)/shard_map/reduce_scatter | solution.py:243
  (233 shorter events, 187.9 us)
Async XLA Ops:
  7.2 33.4 %all-gather.18.cloned.1.call-start = ((), (), s32[]{:S(2)}) async-start(), calls=%async_computation.14 | async-start | bytes 2359296 | tf_op jit(solution)/shard_map/all_gather | solution.py:80
  7.9 115.6 %all-gather.12.cloned.1.call-start = ((), (), s32[]{:S(2)}) async-start(), calls=%async_computation.11 | async-start | bytes 5242880 | tf_op jit(solution)/shard_map/all_gather | solution.py:96
  14.2 137.6 %all-gather.16.cloned.1.call-start = ((), (), s32[]{:S(2)}) async-start(), calls=%async_computation.13 | async-start | bytes 2359296 | tf_op jit(solution)/shard_map/all_gather | solution.py:79
  14.9 166.6 %all-gather.14.cloned.1.call-start = ((), (), s32[]{:S(2)}) async-start(), calls=%async_computation.12 | async-start | bytes 2359296 | tf_op jit(solution)/shard_map/all_gather | solution.py:81
  15.5 196.0 %all-gather.20.cloned.1.call-start = ((), (), s32[]{:S(2)}) async-start(), calls=%async_computation.15 | async-start | bytes 2359296 | tf_op jit(solution)/shard_map/all_gather | solution.py:84
  16.1 347.3 %reduce-scatter.12.cloned.1.call-start = ((), (), s32[]{:S(2)}) async-start(), calls=%async_computation.16 | async-start | bytes 10485760 | tf_op jit(solution)/shard_map/reduce_scatter | solution.py:135
  16.3 173.1 %copy-start.7 = (pred[512,1024]{1,0:T(8,128)(4,1)}, pred[512,1024]{1,0:T(8,128)(4,1)S(1)}, u32[]{:S(2)}) copy-start(pred[512,1024]{1,0:T(8,128)(4,1)S(1)} %iota_compare_fusion.1) | copy-start | bytes 1572868
  16.7 170.2 %copy-start.5 = (pred[512,1024]{1,0:T(8,128)(4,1)}, pred[512,1024]{1,0:T(8,128)(4,1)S(1)}, u32[]{:S(2)}) copy-start(pred[512,1024]{1,0:T(8,128)(4,1)S(1)} %iota_compare_fusion) | copy-start | bytes 1572868
  192.4 26.3 %copy-start.26 = (bf16[1024,4,128]{0,2,1:T(8,128)(2,1)}, bf16[1024,4,128]{0,2,1:T(8,128)(2,1)S(1)}, u32[]{:S(2)}) copy-start(bf16[1024,4,128]{0,2,1:T(8,128)(2,1)S(1)} %pad_maximum_fusion.2) | copy-start | bytes 3145732
  218.7 144.7 %copy-start.3 = (bf16[1,256,2048]{2,1,0:T(8,128)(2,1)S(1)}, bf16[1,256,2048]{2,1,0:T(8,128)(2,1)}, u32[]{:S(2)}) copy-start(bf16[1,256,2048]{2,1,0:T(8,128)(2,1)} %param.10) | copy-start | bytes 3145732
  218.8 201.7 %all-gather.24.cloned.1.call-start = ((), (), s32[]{:S(2)}) async-start(), calls=%async_computation.18 | async-start | bytes 9437184 | tf_op jit(solution)/shard_map/all_gather | solution.py:82
  219.5 283.8 %all-gather.22.cloned.1.call-start = ((), (), s32[]{:S(2)}) async-start(), calls=%async_computation.17 | async-start | bytes 5242880 | tf_op jit(solution)/shard_map/all_gather | solution.py:143
  366.9 191.3 %all-gather.26.cloned.1.call-start = ((), (), s32[]{:S(2)}) async-start(), calls=%async_computation.19 | async-start | bytes 9437184 | tf_op jit(solution)/shard_map/all_gather | solution.py:83
  367.7 248.2 %all-gather.28.cloned.1.call-start = ((), (), s32[]{:S(2)}) async-start(), calls=%async_computation.20 | async-start | bytes 9437184 | tf_op jit(solution)/shard_map/all_gather | solution.py:85
  368.3 338.5 %reduce-scatter.14.cloned.1.call-start = ((), (), s32[]{:S(2)}) async-start(), calls=%async_computation.21 | async-start | bytes 5242880 | tf_op jit(solution)/shard_map/reduce_scatter | solution.py:149
  629.8 77.0 %copy-start.12 = (bf16[1,256,2048]{2,1,0:T(8,128)(2,1)S(1)}, bf16[1,256,2048]{2,1,0:T(8,128)(2,1)}, u32[]{:S(2)}) copy-start(bf16[1,256,2048]{2,1,0:T(8,128)(2,1)} %param.11) | copy-start | bytes 3145732
  629.8 161.1 %all-gather.30.cloned.1.call-start = ((), (), s32[]{:S(2)}) async-start(), calls=%async_computation.22 | async-start | bytes 5242880 | tf_op jit(solution)/shard_map/all_gather | solution.py:171
  709.5 203.4 %reduce-scatter.16.cloned.1.call-start = ((), (), s32[]{:S(2)}) async-start(), calls=%async_computation.23 | async-start | bytes 5242880 | tf_op jit(solution)/shard_map/reduce_scatter | solution.py:185
  837.4 163.6 %all-gather.32.cloned.1.call-start = ((), (), s32[]{:S(2)}) async-start(), calls=%async_computation.24 | async-start | bytes 5242880 | tf_op jit(solution)/shard_map/all_gather | solution.py:189
  919.7 209.8 %reduce-scatter.32.cloned.1.call-start = ((), (), s32[]{:S(2)}) async-start(), calls=%async_computation.32 | async-start | bytes 9437184 | tf_op jit(solution)/shard_map/reduce_scatter | solution.py:266
  933.9 216.0 %reduce-scatter.30.cloned.1.call-start = ((), (), s32[]{:S(2)}) async-start(), calls=%async_computation.31 | async-start | bytes 9437184 | tf_op jit(solution)/shard_map/reduce_scatter | solution.py:260
  948.5 276.0 %reduce-scatter.28.cloned.1.call-start = ((), (), s32[]{:S(2)}) async-start(), calls=%async_computation.30 | async-start | bytes 9437184 | tf_op jit(solution)/shard_map/reduce_scatter | solution.py:257
  962.6 38.5 %copy-start.46 = (bf16[512,2048]{1,0:T(8,128)(2,1)S(1)}, bf16[512,2048]{1,0:T(8,128)(2,1)}, u32[]{:S(2)}) copy-start(bf16[512,2048]{1,0:T(8,128)(2,1)} %all-gather.20.cloned.1.call-done) | copy-start | bytes 6291460
  962.6 306.5 %reduce-scatter.26.cloned.1.call-start = ((), (), s32[]{:S(2)}) async-start(), calls=%async_computation.29 | async-start | bytes 2359296 | tf_op jit(solution)/shard_map/reduce_scatter | solution.py:263
  1009.6 304.1 %reduce-scatter.24.cloned.1.call-start = ((), (), s32[]{:S(2)}) async-start(), calls=%async_computation.28 | async-start | bytes 2359296 | tf_op jit(solution)/shard_map/reduce_scatter | solution.py:254
  1043.4 315.1 %reduce-scatter.20.cloned.1.call-start = ((), (), s32[]{:S(2)}) async-start(), calls=%async_computation.26 | async-start | bytes 2359296 | tf_op jit(solution)/shard_map/reduce_scatter | solution.py:248
  1067.2 335.8 %reduce-scatter.22.cloned.1.call-start = ((), (), s32[]{:S(2)}) async-start(), calls=%async_computation.27 | async-start | bytes 2359296 | tf_op jit(solution)/shard_map/reduce_scatter | solution.py:251
  1075.0 407.2 %reduce-scatter.18.cloned.1.call-start = ((), (), s32[]{:S(2)}) async-start(), calls=%async_computation.25 | async-start | bytes 5242880 | tf_op jit(solution)/shard_map/reduce_scatter | solution.py:243
  1132.2 350.0 %copy-start.4 = (bf16[1,256,2048]{2,1,0:T(8,128)(2,1)S(1)}, bf16[1,256,2048]{2,1,0:T(8,128)(2,1)}, u32[]{:S(2)}) copy-start(bf16[1,256,2048]{2,1,0:T(8,128)(2,1)} %param.10) | copy-start | bytes 3145732
  1132.2 350.0 %copy-start.40 = (f32[256]{0:T(256)S(1)}, f32[256]{0:T(256)}, u32[]{:S(2)}) copy-start(f32[256]{0:T(256)} %copy-done.39) | copy-start | bytes 3076
  1132.2 350.0 %copy-start.42 = (f32[256]{0:T(256)S(1)}, f32[256]{0:T(256)}, u32[]{:S(2)}) copy-start(f32[256]{0:T(256)} %copy-done.41) | copy-start | bytes 3076
  1152.6 331.5 %copy-start.16 = (f32[256,2048]{1,0:T(8,128)S(1)}, f32[256,2048]{1,0:T(8,128)}, u32[]{:S(2)}) copy-start(f32[256,2048]{1,0:T(8,128)} %get-tuple-element.16) | copy-start | bytes 6291460
  (44 other events, 223.3 us)
Sparse Core Ops, SparseCore 0:
  9.9 30.6 all-gather.17
  42.7 80.7 all-gather.11
  125.4 26.4 all-gather.15
  153.6 27.8 all-gather.13
  183.2 28.2 all-gather.19
  218.9 144.4 reduce-scatter.11
  365.3 55.0 all-gather.23
  422.6 80.7 all-gather.21
  505.2 52.9 all-gather.25
  559.9 55.9 all-gather.27
  629.9 76.7 reduce-scatter.13
  709.6 81.2 all-gather.29
  837.6 75.2 reduce-scatter.15
  919.8 81.2 all-gather.31
  1004.4 69.7 reduce-scatter.31
  1077.9 71.8 reduce-scatter.29
  1153.1 71.2 reduce-scatter.27
  1227.9 41.1 reduce-scatter.25
  1272.4 41.2 reduce-scatter.23
  1317.2 41.2 reduce-scatter.19
  1361.7 41.2 reduce-scatter.21
  1405.4 76.7 reduce-scatter.17
where the time goes:
time: 1510 us; the launch traced here: 1500 us
  waiting for transfers between devices  1100 us (73%)
  matrix products  233 us (15%)
  other arithmetic  67.9 us (4%)
  blocking collectives  53.5 us (4%)
  local copies, waits for them, and re-layouts  21.9 us (1%)
  between operations  19.5 us (1%)
    reduce_scatter x1, waiting for transfers between devices, local(): lax.psum_scatter(jnp.dot(attended, out_full, preferred_element_type=jnp.f...  144 us
    all_gather x1, waiting for transfers between devices, local(): features_two = lax.all_gather(normed_two, 'tensor', axis=0, tiled=True)  82.9 us
    all_gather x1, waiting for transfers between devices, local(): features = lax.all_gather(normed, 'tensor', axis=0, tiled=True)  82.9 us
    all_gather x1, waiting for transfers between devices, local(): lax.all_gather(grad_result.astype(jnp.bfloat16), 'tensor', axis=0, tiled=...  81.4 us
    reduce_scatter x1, waiting for transfers between devices, local(): lax.psum_scatter(features_grad.astype(jnp.bfloat16), 'tensor', scatter_di...  77.4 us
    reduce_scatter x1, waiting for transfers between devices, local(): lax.psum_scatter(feature_grad.astype(jnp.bfloat16), 'tensor', scatter_dim...  75.4 us
    reduce_scatter x1, waiting for transfers between devices, local(): lax.psum_scatter(grad_gate.astype(jnp.bfloat16), 'dp', scatter_dimension=...  71.8 us
    reduce_scatter x1, waiting for transfers between devices, local(): lax.psum_scatter(jnp.dot(hidden, down_full, preferred_element_type=jnp.fl...  61.4 us
  transfers between devices with their start and end apart: 22, of which 21 were waited for; matrix products, arithmetic and copies ran while one was open for 16% of the time, Pallas kernels for 0%

commit v1 on v0

--- a/solution.py
+++ b/solution.py
@@ -140,7 +140,15 @@
     )
     residual = rows_in + attn_out
     normed_two = layer_norm(residual).astype(jnp.bfloat16)
-    features_two = lax.all_gather(normed_two, "tensor", axis=0, tiled=True)
+    sides = lax.axis_size("tensor")
+    far_arr = sorted(((rr, (rr + 1) % sides) for rr in range(sides)))
+    piece_next = normed_two
+    log = [piece_next]
+    for hop_no in range(1, sides):
+        piece_next = lax.ppermute(piece_next, "tensor", far_arr)
+        log.insert(0, piece_next)
+    clean = jnp.concatenate(log, 0)
+    features_two = jnp.roll(clean, (lax.axis_index("tensor") + 1) * normed_two.shape[0], 0)
     gate_pre = jnp.dot(features_two, gate_full, preferred_element_type=jnp.float32)
     up_pre = jnp.dot(features_two, up_full, preferred_element_type=jnp.float32)
     gate_sigmoid = jax.nn.sigmoid(gate_pre)

time: 1510 us -> 1430 us (0.947)
  waiting for transfers between devices: 1100 us -> 1000 us
    all_gather x1 -> x0, waiting for transfers between devices: 82.9 us -> none  [local(): features_two = lax.all_gather(normed_two, 'tensor', axis=0, tiled=True)]
    ppermute x0 -> x3, waiting for transfers between devices: none -> 76.1 us  [local(): piece_next = lax.ppermute(piece_next, 'tensor', far_arr)]
    all_gather x1, waiting for transfers between devices: 52.1 us -> 0.01 us  [local(): lax.all_gather(w_gate, 'dp', axis=0, tiled=True)]
    all_gather x1, waiting for transfers between devices: 40 us -> 4.32 us  [local(): lax.all_gather(w_up, 'dp', axis=0, tiled=True)]
  transfers between devices with their start and end apart: 22 -> 24, of which waited for: 21 -> 22; matrix products, arithmetic and copies ran while one was open for 16% -> 18% of each run, Pallas kernels for 0% -> 0%
where the time goes in v1:
time: 1430 us; the launch traced here: 1410 us
  waiting for transfers between devices  1000 us (70%)
  matrix products  233 us (16%)
  other arithmetic  69.4 us (5%)
  blocking collectives  53.3 us (4%)
  local copies, waits for them, and re-layouts  33.7 us (2%)
  between operations  19.4 us (1%)
    reduce_scatter x1, waiting for transfers between devices, local(): lax.psum_scatter(jnp.dot(attended, out_full, preferred_element_type=jnp.f...  142 us
    all_gather x1, waiting for transfers between devices, local(): features = lax.all_gather(normed, 'tensor', axis=0, tiled=True)  82.9 us
    all_gather x1, waiting for transfers between devices, local(): lax.all_gather(grad_result.astype(jnp.bfloat16), 'tensor', axis=0, tiled=...  81.4 us
    reduce_scatter x1, waiting for transfers between devices, local(): lax.psum_scatter(features_grad.astype(jnp.bfloat16), 'tensor', scatter_di...  77.4 us
    ppermute x3, waiting for transfers between devices, local(): piece_next = lax.ppermute(piece_next, 'tensor', far_arr)  76.1 us
    reduce_scatter x1, waiting for transfers between devices, local(): lax.psum_scatter(feature_grad.astype(jnp.bfloat16), 'tensor', scatter_dim...  75.4 us
    reduce_scatter x1, waiting for transfers between devices, local(): lax.psum_scatter(grad_gate.astype(jnp.bfloat16), 'dp', scatter_dimension=...  71.8 us
    reduce_scatter x1, waiting for transfers between devices, local(): lax.psum_scatter(jnp.dot(hidden, down_full, preferred_element_type=jnp.fl...  61.4 us
  transfers between devices with their start and end apart: 24, of which 22 were waited for; matrix products, arithmetic and copies ran while one was open for 18% of the time, Pallas kernels for 0%

profile of v1, /device:TPU:0, one launch (start us, length us, event | category | flops | bytes accessed | tf_op | source)
XLA Modules:
  0.0 1414.6 jit_solution(12315345629122144650)
XLA Ops:
  19.6 21.0 %all-gather.17.cloned.1.call-done = bf16[2048,512]{1,0:T(8,128)(2,1)} async-done(((bf16[256,512]{1,0:T(8,128)(2,1)}), bf16[2048,512]{1,0:T(8,128)(2,1)}) %all-gather.17.cloned.1.call-update) | async-done | bytes 2097168 | tf_op jit(solution)/shard_map/all_gather | solution.py:80
  40.5 82.9 %all-gather.11.cloned.1.call-done = bf16[1024,2048]{1,0:T(8,128)(2,1)} async-done(((bf16[256,2048]{1,0:T(8,128)(2,1)}), bf16[1024,2048]{1,0:T(8,128)(2,1)}) %all-gather.11.cloned.1.call-update) | async-done | bytes 4194320 | tf_op jit(solution)/shard_map/all_gather | solution.py:96
  135.3 16.5 %all-gather.15.cloned.1.call-done = bf16[2048,512]{1,0:T(8,128)(2,1)} async-done(((bf16[256,512]{1,0:T(8,128)(2,1)}), bf16[2048,512]{1,0:T(8,128)(2,1)}) %all-gather.15.cloned.1.call-update) | async-done | bytes 2097168 | tf_op jit(solution)/shard_map/all_gather | solution.py:79
  192.4 19.1 %all-gather.19.cloned.1.call-done = bf16[512,2048]{1,0:T(8,128)(2,1)} async-done(((bf16[512,256]{1,0:T(8,128)(2,1)}), bf16[512,2048]{1,0:T(8,128)(2,1)}) %all-gather.19.cloned.1.call-update) | async-done | bytes 2097168 | tf_op jit(solution)/shard_map/all_gather | solution.py:84
  221.0 142.3 %reduce-scatter.12.cloned.1.call-done = f32[256,2048]{1,0:T(8,128)} async-done(((f32[1024,2048]{1,0:T(8,128)}), f32[256,2048]{1,0:T(8,128)}) %reduce-scatter.12.cloned.1.call-update) | async-done | bytes 2097168 | tf_op jit(solution)/shard_map/reduce_scatter | solution.py:135
  367.2 25.3 %collective-permute-done = bf16[256,2048]{1,0:T(8,128)(2,1)S(1)} collective-permute-done((bf16[256,2048]{1,0:T(8,128)(2,1)S(1)}, bf16[256,2048]{1,0:T(8,128)(2,1)S(1)}, u32[]{:S(2)}, u32[]{:S(2)}) %collective-permute-start) | collective-permute-done | bytes 1048608 | tf_op jit(solution)/shard_map/ppermute | solution.py:148
  392.5 25.7 %collective-permute-done.1 = bf16[256,2048]{1,0:T(8,128)(2,1)} collective-permute-done((bf16[256,2048]{1,0:T(8,128)(2,1)S(1)}, bf16[256,2048]{1,0:T(8,128)(2,1)}, u32[]{:S(2)}, u32[]{:S(2)}) %collective-permute-start.1) | collective-permute-done | bytes 1048608 | tf_op jit(solution)/shard_map/ppermute | solution.py:148
  418.3 25.0 %collective-permute-done.2 = bf16[256,2048]{1,0:T(8,128)(2,1)} collective-permute-done((bf16[256,2048]{1,0:T(8,128)(2,1)}, bf16[256,2048]{1,0:T(8,128)(2,1)}, u32[]{:S(2)}, u32[]{:S(2)}) %collective-permute-start.2) | collective-permute-done | bytes 1048608 | tf_op jit(solution)/shard_map/ppermute | solution.py:148
  457.6 14.8 %fusion.21 = f32[1024,2048]{1,0:T(8,128)} fusion(bf16[2048,2048]{1,0:T(8,128)(2,1)} %all-gather.21.cloned.1.call-done, bf16[2048,2048]{1,0:T(8,128)(2,1)} %constant_dynamic-update-slice_fusion, s32[]{:T(128)S(6)} %select_n.29), kind=kOutput, calls=%fused_computation.51 | convolution fusion | flops 8589934592 | bytes 20971524 | tf_op jit(solution)/shard_map/dot_general | solution.py:152
  476.7 17.3 %multiply_convert_fusion.4 = (bf16[1024,2048]{1,0:T(8,128)(2,1)}, f32[1024,2048]{1,0:T(8,128)}) fusion(f32[1024,2048]{1,0:T(8,128)} %fusion.21, bf16[2048,2048]{1,0:T(8,128)(2,1)} %all-gather.23.cloned.1.call-done, bf16[2048,2048]{1,0:T(8,128)(2,1)} %constant_dynamic-update-slice_fusion, s32[]{:T(128)S(6)} %select_n.29), kind=kOutput, calls=%fused_computation.10 | convolution fusion | flops 8602517504 | bytes 33554436 | tf_op jit(solution)/shard_map/dot_general | solution.py:153
  494.0 40.6 %all-gather.25.cloned.1.call-done = bf16[2048,2048]{1,0:T(8,128)(2,1)} async-done(((bf16[2048,256]{1,0:T(8,128)(2,1)}), bf16[2048,2048]{1,0:T(8,128)(2,1)}) %all-gather.25.cloned.1.call-update) | async-done | bytes 8388624 | tf_op jit(solution)/shard_map/all_gather | solution.py:85
  534.6 13.9 convolution_convert_fusion.3
  549.3 14.0 psum.15
  564.0 61.4 %reduce-scatter.14.cloned.1.call-done = bf16[256,2048]{1,0:T(8,128)(2,1)} async-done(((bf16[1024,2048]{1,0:T(8,128)(2,1)}), bf16[256,2048]{1,0:T(8,128)(2,1)}) %reduce-scatter.14.cloned.1.call-update) | async-done | bytes 1048592 | tf_op jit(solution)/shard_map/reduce_scatter | solution.py:157
  628.2 81.4 %all-gather.27.cloned.1.call-done = bf16[1024,2048]{1,0:T(8,128)(2,1)} async-done(((bf16[256,2048]{1,0:T(8,128)(2,1)}), bf16[1024,2048]{1,0:T(8,128)(2,1)}) %all-gather.27.cloned.1.call-update) | async-done | bytes 4194320 | tf_op jit(solution)/shard_map/all_gather | solution.py:179
  709.6 20.8 %multiply_convert_fusion.2 = (bf16[1024,2048]{1,0:T(8,128)(2,1)}, bf16[1024,2048]{1,0:T(8,128)(2,1)}) fusion(f32[1024,2048]{1,0:T(8,128)} %fusion.21, f32[1024,2048]{1,0:T(8,128)} %get-tuple-element.47, bf16[1024,2048]{1,0:T(8,128)(2,1)} %all-gather.27.cloned.1.call-done, bf16[2048,2048]{1,0:T(8,128)(2,1)} %all-gather.25.cloned.1.call-done), kind=kOutput, calls=%fused_computation.8 | convolution fusion | flops 8617197568 | bytes 37748736 | tf_op jit(solution)/shard_map/td,fd->tf/dot_general | solution.py:181
  730.4 12.7 fusion.78
  743.1 13.1 add_convert_fusion.1
  756.2 75.4 %reduce-scatter.16.cloned.1.call-done = bf16[256,2048]{1,0:T(8,128)(2,1)} async-done(((bf16[1024,2048]{1,0:T(8,128)(2,1)}), bf16[256,2048]{1,0:T(8,128)(2,1)}) %reduce-scatter.16.cloned.1.call-update) | async-done | bytes 1048592 | tf_op jit(solution)/shard_map/reduce_scatter | solution.py:193
  838.5 14.1 convolution_convert_fusion
  852.7 14.2 %convolution_convert_fusion.1 = bf16[2048,2048]{1,0:T(8,128)(2,1)} fusion(bf16[1024,2048]{1,0:T(8,128)(2,1)} %get-tuple-element.19, bf16[2048,2048]{1,0:T(8,128)(2,1)} %constant_dynamic-update-slice_fusion, s32[]{:T(128)S(6)} %select_n.29), kind=kOutput, calls=%fused_computation.18 | convolution fusion | flops 8594128896 | bytes 16777220 | tf_op jit(solution)/shard_map/td,tf->df/dot_general | solution.py:189
  867.0 14.0 convolution_convert_fusion.2
  881.7 38.1 %all-gather.29.cloned.1.call-done = bf16[1024,2048]{1,0:T(8,128)(2,1)} async-done(((bf16[256,2048]{1,0:T(8,128)(2,1)}), bf16[1024,2048]{1,0:T(8,128)(2,1)}) %all-gather.29.cloned.1.call-update) | async-done | bytes 4194320 | tf_op jit(solution)/shard_map/all_gather | solution.py:197
  954.4 7.9 multiply_reduce_fusion
  1008.3 39.2 %psum.14 = f32[]{:T(128)} all-reduce(f32[]{:T(128)} %get-tuple-element.11), channel_id=1, replica_groups=mesh['dp'=8,'tensor'=4] {'dp','tensor'}, use_global_device_ids=true, to_apply=%region_11.12 | all-reduce | flops 1 | bytes 8 | tf_op jit(solution)/shard_map/psum | solution.py:166
  1051.0 17.7 %reduce-scatter.30.cloned.1.call-done = bf16[256,2048]{1,0:T(8,128)(2,1)} async-done(((bf16[2048,2048]{1,0:T(8,128)(2,1)}), bf16[256,2048]{1,0:T(8,128)(2,1)}) %reduce-scatter.30.cloned.1.call-update) | async-done | bytes 1048592 | tf_op jit(solution)/shard_map/reduce_scatter | solution.py:268
  1071.4 71.8 %reduce-scatter.28.cloned.1.call-done = bf16[256,2048]{1,0:T(8,128)(2,1)} async-done(((bf16[2048,2048]{1,0:T(8,128)(2,1)}), bf16[256,2048]{1,0:T(8,128)(2,1)}) %reduce-scatter.28.cloned.1.call-update) | async-done | bytes 1048592 | tf_op jit(solution)/shard_map/reduce_scatter | solution.py:265
  1146.0 42.0 %reduce-scatter.26.cloned.1.call-done = bf16[512,256]{1,0:T(8,128)(2,1)} async-done(((bf16[512,2048]{1,0:T(8,128)(2,1)}), bf16[512,256]{1,0:T(8,128)(2,1)}) %reduce-scatter.26.cloned.1.call-update) | async-done | bytes 262160 | tf_op jit(solution)/shard_map/reduce_scatter | solution.py:271
  1189.8 42.6 %reduce-scatter.24.cloned.1.call-done = bf16[256,512]{1,0:T(8,128)(2,1)} async-done(((bf16[2048,512]{1,0:T(8,128)(2,1)}), bf16[256,512]{1,0:T(8,128)(2,1)}) %reduce-scatter.24.cloned.1.call-update) | async-done | bytes 262160 | tf_op jit(solution)/shard_map/reduce_scatter | solution.py:262
  1234.2 43.1 %reduce-scatter.20.cloned.1.call-done = bf16[256,512]{1,0:T(8,128)(2,1)} async-done(((bf16[2048,512]{1,0:T(8,128)(2,1)}), bf16[256,512]{1,0:T(8,128)(2,1)}) %reduce-scatter.20.cloned.1.call-update) | async-done | bytes 262160 | tf_op jit(solution)/shard_map/reduce_scatter | solution.py:256
  1279.1 42.6 %reduce-scatter.22.cloned.1.call-done = bf16[256,512]{1,0:T(8,128)(2,1)} async-done(((bf16[2048,512]{1,0:T(8,128)(2,1)}), bf16[256,512]{1,0:T(8,128)(2,1)}) %reduce-scatter.22.cloned.1.call-update) | async-done | bytes 262160 | tf_op jit(solution)/shard_map/reduce_scatter | solution.py:259
  1323.5 77.4 %reduce-scatter.18.cloned.1.call-done = bf16[256,2048]{1,0:T(8,128)(2,1)} async-done(((bf16[1024,2048]{1,0:T(8,128)(2,1)}), bf16[256,2048]{1,0:T(8,128)(2,1)}) %reduce-scatter.18.cloned.1.call-update) | async-done | bytes 1048592 | tf_op jit(solution)/shard_map/reduce_scatter | solution.py:251
  (244 shorter events, 207.1 us)
Async XLA Ops:
  7.2 33.4 %all-gather.17.cloned.1.call-start = ((), (), s32[]{:S(2)}) async-start(), calls=%async_computation.14 | async-start | bytes 2359296 | tf_op jit(solution)/shard_map/all_gather | solution.py:80
  7.9 115.6 %all-gather.11.cloned.1.call-start = ((), (), s32[]{:S(2)}) async-start(), calls=%async_computation.11 | async-start | bytes 5242880 | tf_op jit(solution)/shard_map/all_gather | solution.py:96
  14.2 137.6 %all-gather.15.cloned.1.call-start = ((), (), s32[]{:S(2)}) async-start(), calls=%async_computation.13 | async-start | bytes 2359296 | tf_op jit(solution)/shard_map/all_gather | solution.py:79
  14.9 166.6 %all-gather.13.cloned.1.call-start = ((), (), s32[]{:S(2)}) async-start(), calls=%async_computation.12 | async-start | bytes 2359296 | tf_op jit(solution)/shard_map/all_gather | solution.py:81
  15.5 196.0 %all-gather.19.cloned.1.call-start = ((), (), s32[]{:S(2)}) async-start(), calls=%async_computation.15 | async-start | bytes 2359296 | tf_op jit(solution)/shard_map/all_gather | solution.py:84
  16.1 347.3 %reduce-scatter.12.cloned.1.call-start = ((), (), s32[]{:S(2)}) async-start(), calls=%async_computation.16 | async-start | bytes 10485760 | tf_op jit(solution)/shard_map/reduce_scatter | solution.py:135
  16.3 173.1 %copy-start.7 = (pred[512,1024]{1,0:T(8,128)(4,1)}, pred[512,1024]{1,0:T(8,128)(4,1)S(1)}, u32[]{:S(2)}) copy-start(pred[512,1024]{1,0:T(8,128)(4,1)S(1)} %iota_compare_fusion.1) | copy-start | bytes 1572868
  16.7 170.2 %copy-start.5 = (pred[512,1024]{1,0:T(8,128)(4,1)}, pred[512,1024]{1,0:T(8,128)(4,1)S(1)}, u32[]{:S(2)}) copy-start(pred[512,1024]{1,0:T(8,128)(4,1)S(1)} %iota_compare_fusion) | copy-start | bytes 1572868
  218.7 144.7 %copy-start.3 = (bf16[1,256,2048]{2,1,0:T(8,128)(2,1)S(1)}, bf16[1,256,2048]{2,1,0:T(8,128)(2,1)}, u32[]{:S(2)}) copy-start(bf16[1,256,2048]{2,1,0:T(8,128)(2,1)} %param.10) | copy-start | bytes 3145732
  218.8 238.9 %all-gather.21.cloned.1.call-start = ((), (), s32[]{:S(2)}) async-start(), calls=%async_computation.17 | async-start | bytes 9437184 | tf_op jit(solution)/shard_map/all_gather | solution.py:82
  219.5 257.2 %all-gather.23.cloned.1.call-start = ((), (), s32[]{:S(2)}) async-start(), calls=%async_computation.18 | async-start | bytes 9437184 | tf_op jit(solution)/shard_map/all_gather | solution.py:83
  220.3 314.3 %all-gather.25.cloned.1.call-start = ((), (), s32[]{:S(2)}) async-start(), calls=%async_computation.19 | async-start | bytes 9437184 | tf_op jit(solution)/shard_map/all_gather | solution.py:85
  221.0 404.4 %reduce-scatter.14.cloned.1.call-start = ((), (), s32[]{:S(2)}) async-start(), calls=%async_computation.20 | async-start | bytes 5242880 | tf_op jit(solution)/shard_map/reduce_scatter | solution.py:157
  365.9 26.6 %collective-permute-start = (bf16[256,2048]{1,0:T(8,128)(2,1)S(1)}, bf16[256,2048]{1,0:T(8,128)(2,1)S(1)}, u32[]{:S(2)}, u32[]{:S(2)}) collective-permute-start(bf16[256,2048]{1,0:T(8,128)(2,1)S(1)} %fusion.42), channel_id=1, source_target_pairs={{0,1},{1,2},{2,3},{3,0},{4,5},{5,6},{6,7},{7,4},{8,9},{9,10},{10,1... | collective-permute-start | bytes 3145736 | tf_op jit(solution)/shard_map/ppermute | solution.py:148
  392.5 25.7 %collective-permute-start.1 = (bf16[256,2048]{1,0:T(8,128)(2,1)S(1)}, bf16[256,2048]{1,0:T(8,128)(2,1)}, u32[]{:S(2)}, u32[]{:S(2)}) collective-permute-start(bf16[256,2048]{1,0:T(8,128)(2,1)S(1)} %collective-permute-done), channel_id=1, source_target_pairs={{0,1},{1,2},{2,3},{3,0},{4,5},{5,6},{6,7},{7,4},{8,9},{9,10},{10,1... | collective-permute-start | bytes 3145736 | tf_op jit(solution)/shard_map/ppermute | solution.py:148
  418.3 25.0 %collective-permute-start.2 = (bf16[256,2048]{1,0:T(8,128)(2,1)}, bf16[256,2048]{1,0:T(8,128)(2,1)}, u32[]{:S(2)}, u32[]{:S(2)}) collective-permute-start(bf16[256,2048]{1,0:T(8,128)(2,1)} %collective-permute-done.1), channel_id=1, source_target_pairs={{0,1},{1,2},{2,3},{3,0},{4,5},{5,6},{6,7},{7,4},{8,9},{9,10},{10,1... | collective-permute-start | bytes 3145736 | tf_op jit(solution)/shard_map/ppermute | solution.py:148
  548.5 77.0 %copy-start.12 = (bf16[1,256,2048]{2,1,0:T(8,128)(2,1)S(1)}, bf16[1,256,2048]{2,1,0:T(8,128)(2,1)}, u32[]{:S(2)}) copy-start(bf16[1,256,2048]{2,1,0:T(8,128)(2,1)} %param.11) | copy-start | bytes 3145732
  548.5 161.1 %all-gather.27.cloned.1.call-start = ((), (), s32[]{:S(2)}) async-start(), calls=%async_computation.21 | async-start | bytes 5242880 | tf_op jit(solution)/shard_map/all_gather | solution.py:179
  628.2 203.5 %reduce-scatter.16.cloned.1.call-start = ((), (), s32[]{:S(2)}) async-start(), calls=%async_computation.22 | async-start | bytes 5242880 | tf_op jit(solution)/shard_map/reduce_scatter | solution.py:193
  756.2 163.7 %all-gather.29.cloned.1.call-start = ((), (), s32[]{:S(2)}) async-start(), calls=%async_computation.23 | async-start | bytes 5242880 | tf_op jit(solution)/shard_map/all_gather | solution.py:197
  838.5 209.8 %reduce-scatter.32.cloned.1.call-start = ((), (), s32[]{:S(2)}) async-start(), calls=%async_computation.31 | async-start | bytes 9437184 | tf_op jit(solution)/shard_map/reduce_scatter | solution.py:274
  852.7 216.0 %reduce-scatter.30.cloned.1.call-start = ((), (), s32[]{:S(2)}) async-start(), calls=%async_computation.30 | async-start | bytes 9437184 | tf_op jit(solution)/shard_map/reduce_scatter | solution.py:268
  866.9 276.3 %reduce-scatter.28.cloned.1.call-start = ((), (), s32[]{:S(2)}) async-start(), calls=%async_computation.29 | async-start | bytes 9437184 | tf_op jit(solution)/shard_map/reduce_scatter | solution.py:265
  881.0 307.0 %reduce-scatter.26.cloned.1.call-start = ((), (), s32[]{:S(2)}) async-start(), calls=%async_computation.28 | async-start | bytes 2359296 | tf_op jit(solution)/shard_map/reduce_scatter | solution.py:271
  928.5 303.9 %reduce-scatter.24.cloned.1.call-start = ((), (), s32[]{:S(2)}) async-start(), calls=%async_computation.27 | async-start | bytes 2359296 | tf_op jit(solution)/shard_map/reduce_scatter | solution.py:262
  962.4 314.9 %reduce-scatter.20.cloned.1.call-start = ((), (), s32[]{:S(2)}) async-start(), calls=%async_computation.25 | async-start | bytes 2359296 | tf_op jit(solution)/shard_map/reduce_scatter | solution.py:256
  986.2 335.5 %reduce-scatter.22.cloned.1.call-start = ((), (), s32[]{:S(2)}) async-start(), calls=%async_computation.26 | async-start | bytes 2359296 | tf_op jit(solution)/shard_map/reduce_scatter | solution.py:259
  994.0 406.9 %reduce-scatter.18.cloned.1.call-start = ((), (), s32[]{:S(2)}) async-start(), calls=%async_computation.24 | async-start | bytes 5242880 | tf_op jit(solution)/shard_map/reduce_scatter | solution.py:251
  1051.0 349.9 %copy-start.4 = (bf16[1,256,2048]{2,1,0:T(8,128)(2,1)S(1)}, bf16[1,256,2048]{2,1,0:T(8,128)(2,1)}, u32[]{:S(2)}) copy-start(bf16[1,256,2048]{2,1,0:T(8,128)(2,1)} %param.10) | copy-start | bytes 3145732
  1051.0 349.9 %copy-start.40 = (f32[256]{0:T(256)S(1)}, f32[256]{0:T(256)}, u32[]{:S(2)}) copy-start(f32[256]{0:T(256)} %copy-done.39) | copy-start | bytes 3076
  1051.0 349.9 %copy-start.42 = (f32[256]{0:T(256)S(1)}, f32[256]{0:T(256)}, u32[]{:S(2)}) copy-start(f32[256]{0:T(256)} %copy-done.41) | copy-start | bytes 3076
  1071.4 331.4 %copy-start.16 = (f32[256,2048]{1,0:T(8,128)S(1)}, f32[256,2048]{1,0:T(8,128)}, u32[]{:S(2)}) copy-start(f32[256,2048]{1,0:T(8,128)} %get-tuple-element.16) | copy-start | bytes 6291460
  (46 other events, 289.1 us)
Sparse Core Ops, SparseCore 0:
  9.9 30.5 all-gather.16
  42.7 80.7 all-gather.10
  125.4 26.4 all-gather.14
  153.6 27.8 all-gather.12
  183.2 28.2 all-gather.18
  218.9 144.4 reduce-scatter.11
  365.3 55.0 all-gather.20
  422.3 54.3 all-gather.22
  478.6 55.9 all-gather.24
  548.6 76.7 reduce-scatter.13
  628.3 81.2 all-gather.26
  756.3 75.2 reduce-scatter.15
  838.6 81.2 all-gather.28
  923.2 69.8 reduce-scatter.31
  996.7 71.8 reduce-scatter.29
  1072.0 71.2 reduce-scatter.27
  1146.7 41.2 reduce-scatter.25
  1191.1 41.2 reduce-scatter.23
  1236.0 41.2 reduce-scatter.19
  1280.4 41.1 reduce-scatter.21
  1324.1 76.7 reduce-scatter.17
